TPU v7x, 32 devices: a whole 2x2x4 slice. The times are simulated.
32 devices in a mesh: row: 16 (over z, x, core), col: 2 (over y).
Axes of the slice: x: 2, y: 2, z: 4, core: 2. Of those that a mesh axis runs over, the one named last changes fastest.
Arguments:
- counts: float32 [8192, 8192], P('row', 'col'), may hold values from 0 to 12, as said below
- loadings: float32 [8192, 64], P(('col', 'row')), may hold values from 0.02 to 0.4
Outputs:
- row_grad: float32 [8192, 64], P(('row', 'col'))
- col_grad: float32 [8192, 64], P(('col', 'row'))
Inputs may be any that keep to these rules, and one draw needn't show every extreme that they name: `counts`: whole numbers, more of them near the diagonal.
All inputs are finite; a program needn't handle non-finite values.
Results may differ from a plain program's by a relative error of at most 0.0003.
Values sent between devices are 32-bit elements; how exact they have to be, the bound alone decides.
A program may use at most 64 MiB of HBM per device.

v0:
```python
import jax
import jax.numpy as jnp
from jax import lax
from jax.sharding import PartitionSpec as P


def broadcast(block, axis, source):
    block = jnp.where(lax.axis_index(axis) == source, block, jnp.zeros_like(block))
    return lax.psum(block, axis)


def shards(counts, loadings):
    rows = counts.shape[0]
    cols = counts.shape[1]
    nrow = lax.axis_size("row")
    ncol = lax.axis_size("col")
    nbins = rows * nrow
    scale = 1.0 / nbins**0.5
    row_index = lax.axis_index("row")
    col_index = lax.axis_index("col")
    colblock = lax.all_gather(loadings, "row", axis=0, tiled=True)
    group = nrow // ncol
    offset = row_index % group * rows
    portion = lax.dynamic_slice_in_dim(colblock, offset, rows, 0)
    rowblock = broadcast(portion, "col", row_index // group)
    rate = jnp.dot(rowblock, colblock.T, precision=lax.Precision.HIGHEST)
    positions = row_index * rows + jnp.arange(rows)
    targets = col_index * cols + jnp.arange(cols)
    keep = jnp.abs(positions[:, None] - targets[None, :]) >= 2
    ratio = jnp.where(keep, 1.0 - counts / rate, jnp.float32(0.0))
    slab = ratio
    row_grad = lax.psum_scatter(
        jnp.dot(slab, colblock, precision=lax.Precision.HIGHEST) * scale,
        "col",
        scatter_dimension=0,
        tiled=True,
    )
    slab = ratio
    col_grad = lax.psum_scatter(
        jnp.einsum("ij,ik->jk", slab, rowblock, precision=lax.Precision.HIGHEST) * scale,
        "row",
        scatter_dimension=0,
        tiled=True,
    )
    return (row_grad, col_grad)


def solution(mesh):
    placed = (P("row", "col"), P(("col", "row"), None))
    return jax.shard_map(
        shards,
        mesh=mesh,
        in_specs=placed,
        out_specs=(P(("row", "col"), None), P(("col", "row"), None)),
        check_vma=False,
    )
```

profile of v0, /device:TPU:0, one launch (start us, length us, event | category | flops | bytes accessed | tf_op | source)
XLA Modules:
  0.0 175.3 jit_solution(6677871117199778213)
XLA Ops:
  7.2 0.0 all-gather.2.cloned.1.call-start
  7.2 0.7 all-gather.2.cloned.1.call-update
  7.9 0.0 all-reduce.2.cloned.1.call-start
  8.0 41.6 %all-gather.2.cloned.1.call-done = f32[4096,64]{0,1:T(8,128)} async-done(((f32[256,64]{0,1:T(8,128)}), f32[4096,64]{0,1:T(8,128)}) %all-gather.2.cloned.1.call-update) | async-done | bytes 1048592 | tf_op jit(solution)/shard_map/all_gather | solution.py:21
  49.5 1.6 dynamic-slice_select_fusion
  51.1 0.0 all-reduce.2.cloned.1.call-update
  51.1 0.0 reduce-scatter.3.cloned.1.call-start
  51.2 0.0 copy-start.1
  51.2 21.7 %all-reduce.2.cloned.1.call-done = f32[512,64]{0,1:T(8,128)} async-done(((f32[512,64]{0,1:T(8,128)}), f32[512,64]{0,1:T(8,128)}) %all-reduce.2.cloned.1.call-update) | async-done | bytes 131088 | tf_op jit(solution)/shard_map/psum | solution.py:9
  73.0 11.5 %subtract_select_fusion = f32[512,4096]{1,0:T(8,128)S(1)} fusion(f32[512,4096]{1,0:T(8,128)} %param.2, f32[512,64]{0,1:T(8,128)} %all-reduce.2.cloned.1.call-done, f32[4096,64]{0,1:T(8,128)} %all-gather.2.cloned.1.call-done, s32[4096]{0:T(1024)S(1)} %iota_add_fusion, s32[512]{0:T(512)S(1)} %iota_add_fusion.1), kind=kOutput, calls=%fused_computation | convolution fusion | flops 1623195648 | bytes 17975296 | tf_op jit(solution)/shard_map/dot_general | solution.py:26
  84.5 0.0 copy-start
  84.5 3.2 %copy-done = f32[512,4096]{1,0:T(8,128)} copy-done((f32[512,4096]{1,0:T(8,128)}, f32[512,4096]{1,0:T(8,128)S(1)}, u32[]{:S(2)}) %copy-start) | copy-done | bytes 8388632
  87.7 0.0 copy-done.1
  87.7 0.0 copy-start.2
  87.7 8.9 %convolution_multiply_fusion.1 = f32[512,64]{0,1:T(8,128)} fusion(f32[512,4096]{1,0:T(8,128)S(1)} %subtract_select_fusion, f32[4096,64]{0,1:T(8,128)S(1)} %copy-done.1), kind=kOutput, calls=%fused_computation.3 | convolution fusion | flops 1610645504 | bytes 9568256 | tf_op jit(solution)/shard_map/dot_general | solution.py:33
  96.6 0.0 reduce-scatter.3.cloned.1.call-update
  96.6 0.2 reduce-scatter.5.cloned.1.call-start
  96.8 0.0 copy-done.2
  96.8 9.0 %convolution_multiply_fusion = f32[4096,64]{0,1:T(8,128)} fusion(f32[512,4096]{1,0:T(8,128)} %copy-done, f32[512,64]{0,1:T(8,128)S(1)} %copy-done.2), kind=kOutput, calls=%fused_computation.2 | convolution fusion | flops 1610874880 | bytes 9568256 | tf_op jit(solution)/shard_map/ij,ik->jk/dot_general | solution.py:40
  105.9 0.0 reduce-scatter.5.cloned.1.call-update
  105.9 1.2 reduce-scatter.3.cloned.1.call-done
  107.1 61.6 %reduce-scatter.5.cloned.1.call-done = f32[256,64]{0,1:T(8,128)} async-done(((f32[4096,64]{0,1:T(8,128)}), f32[256,64]{0,1:T(8,128)}) %reduce-scatter.5.cloned.1.call-update) | async-done | bytes 65552 | tf_op jit(solution)/shard_map/reduce_scatter | solution.py:39
  (2 shorter events, 0.0 us)
Async XLA Ops:
  7.2 42.4 %all-gather.2.cloned.1.call-start = ((), (), s32[]{:S(2)}) async-start(), calls=%async_computation.2 | async-start | bytes 1114112 | tf_op jit(solution)/shard_map/all_gather | solution.py:21
  7.9 65.1 %all-reduce.2.cloned.1.call-start = ((), (), s32[]{:S(2)}) async-start(), calls=%async_computation.3 | async-start | bytes 262144 | tf_op jit(solution)/shard_map/psum | solution.py:9
  51.1 56.0 %reduce-scatter.3.cloned.1.call-start = ((), (), s32[]{:S(2)}) async-start(), calls=%async_computation.4 | async-start | bytes 196608 | tf_op jit(solution)/shard_map/reduce_scatter | solution.py:32
  51.2 36.5 %copy-start.1 = (f32[4096,64]{0,1:T(8,128)S(1)}, f32[4096,64]{0,1:T(8,128)}, u32[]{:S(2)}) copy-start(f32[4096,64]{0,1:T(8,128)} %all-gather.2.cloned.1.call-done) | copy-start | bytes 3145732
  84.5 3.2 %copy-start = (f32[512,4096]{1,0:T(8,128)}, f32[512,4096]{1,0:T(8,128)S(1)}, u32[]{:S(2)}) copy-start(f32[512,4096]{1,0:T(8,128)S(1)} %subtract_select_fusion) | copy-start | bytes 25165828
  87.7 9.1 %copy-start.2 = (f32[512,64]{0,1:T(8,128)S(1)}, f32[512,64]{0,1:T(8,128)}, u32[]{:S(2)}) copy-start(f32[512,64]{0,1:T(8,128)} %all-reduce.2.cloned.1.call-done) | copy-start | bytes 393220
  96.6 72.2 %reduce-scatter.5.cloned.1.call-start = ((), (), s32[]{:S(2)}) async-start(), calls=%async_computation.5 | async-start | bytes 1114112 | tf_op jit(solution)/shard_map/reduce_scatter | solution.py:39
Sparse Core Ops, SparseCore 0:
  10.1 39.3 all-gather.1
  51.8 21.1 all-reduce.1
  96.7 10.3 reduce-scatter.2
  111.2 57.5 reduce-scatter.4
where the time goes:
time: 175 us
  waiting for transfers between devices  127 us (73%)
  matrix products  29.4 us (17%)
  between operations  13.8 us (8%)
  local copies, waits for them, and re-layouts  3.22 us (2%)
    reduce_scatter x1, waiting for transfers between devices, shards(): lax.psum_scatter(jnp.einsum('ij,ik->jk', slab, rowblock, precision=lax.Pr...  61.6 us
    all_gather x1, waiting for transfers between devices, shards(): colblock = lax.all_gather(loadings, 'row', axis=0, tiled=True)  41.6 us
    psum x1, waiting for transfers between devices, broadcast(): return lax.psum(block, axis)  21.7 us
    dot_general x1, matrix products, shards(): rate = jnp.dot(rowblock, colblock.T, precision=lax.Precision.HIGHEST)  11.5 us
    dot_general x1, matrix products, shards(): jnp.einsum('ij,ik->jk', slab, rowblock, precision=lax.Precision.HIGHEST)  9.02 us
    dot_general x1, matrix products, shards(): jnp.dot(slab, colblock, precision=lax.Precision.HIGHEST) * scale  8.88 us
  transfers between devices with their start and end apart: 4, of which 4 were waited for; matrix products, arithmetic and copies ran while one was open for 5% of the time, Pallas kernels for 0%

commit v1 on v0

--- a/solution.py
+++ b/solution.py
@@ -6,7 +6,7 @@
 
 def broadcast(block, axis, source):
     block = jnp.where(lax.axis_index(axis) == source, block, jnp.zeros_like(block))
-    return lax.psum(block, axis)
+    return jnp.sum(lax.all_gather(block, axis), axis=0)
 
 
 def shards(counts, loadings):

time: 175 us -> 160 us (0.914)
  waiting for transfers between devices: 127 us -> 105 us
  blocking collectives: 0 us -> 6.31 us
    psum x1 -> x0, waiting for transfers between devices: 21.7 us -> none  [broadcast(): return lax.psum(block, axis)]
    all_gather x0 -> x1, blocking collectives: none -> 6.31 us  [broadcast(): return jnp.sum(lax.all_gather(block, axis), axis=0)]
  transfers between devices with their start and end apart: 4 -> 3, of which waited for: 4 -> 3; matrix products, arithmetic and copies ran while one was open for 5% -> 6% of each run, Pallas kernels for 0% -> 0%
where the time goes in v1:
time: 160 us
  waiting for transfers between devices  105 us (66%)
  matrix products  29.5 us (18%)
  between operations  13.8 us (9%)
  blocking collectives  6.31 us (4%)
  local copies, waits for them, and re-layouts  3.44 us (2%)
    reduce_scatter x1, waiting for transfers between devices, shards(): lax.psum_scatter(jnp.einsum('ij,ik->jk', slab, rowblock, precision=lax.Pr...  61.8 us
    all_gather x1, waiting for transfers between devices, shards(): colblock = lax.all_gather(loadings, 'row', axis=0, tiled=True)  41.5 us
    dot_general x1, matrix products, shards(): rate = jnp.dot(rowblock, colblock.T, precision=lax.Precision.HIGHEST)  11.6 us
    dot_general x1, matrix products, shards(): jnp.einsum('ij,ik->jk', slab, rowblock, precision=lax.Precision.HIGHEST)  9 us
    dot_general x1, matrix products, shards(): jnp.dot(slab, colblock, precision=lax.Precision.HIGHEST) * scale  8.92 us
    all_gather x1, blocking collectives, broadcast(): return jnp.sum(lax.all_gather(block, axis), axis=0)  6.31 us
    unnamed x4, local copies, waits for them, and re-layouts  3.22 us
  transfers between devices with their start and end apart: 3, of which 3 were waited for; matrix products, arithmetic and copies ran while one was open for 6% of the time, Pallas kernels for 0%

profile of v1, /device:TPU:0, one launch (start us, length us, event | category | flops | bytes accessed | tf_op | source)
XLA Modules:
  0.0 159.6 jit_solution(16490301196389030746)
XLA Ops:
  7.2 0.0 all-gather.3.cloned.1.call-start
  7.2 0.7 all-gather.3.cloned.1.call-update
  7.9 0.0 reduce-scatter.3.cloned.1.call-start
  8.0 41.5 %all-gather.3.cloned.1.call-done = f32[4096,64]{0,1:T(8,128)} async-done(((f32[256,64]{0,1:T(8,128)}), f32[4096,64]{0,1:T(8,128)}) %all-gather.3.cloned.1.call-update) | async-done | bytes 1048592 | tf_op jit(solution)/shard_map/all_gather | solution.py:21
  49.5 0.9 dynamic-slice_select_fusion
  50.4 6.3 %all-gather = f32[1024,64]{0,1:T(8,128)S(1)} all-gather(f32[512,64]{0,1:T(8,128)S(1)} %dynamic-slice_select_fusion), channel_id=2, replica_groups=mesh['row'=16,'col'=2] {'col'}, dimensions={0}, use_global_device_ids=true | all-gather | bytes 393216 | tf_op jit(solution)/shard_map/all_gather | solution.py:9
  56.8 0.2 reshape.12
  57.0 0.3 reduce_sum.9
  57.3 0.0 copy-start.1
  57.3 11.6 %subtract_select_fusion = f32[512,4096]{1,0:T(8,128)S(1)} fusion(f32[512,4096]{1,0:T(8,128)} %param.2, f32[512,64]{0,1:T(8,128)S(1)} %reduce_sum.9, f32[4096,64]{0,1:T(8,128)} %all-gather.3.cloned.1.call-done, s32[4096]{0:T(1024)S(1)} %iota_add_fusion, s32[512]{0:T(512)S(1)} %iota_add_fusion.1), kind=kOutput, calls=%fused_computation | convolution fusion | flops 1623195648 | bytes 17975296 | tf_op jit(solution)/shard_map/dot_general | solution.py:26
  68.9 0.0 copy-start
  68.9 3.2 %copy-done = f32[512,4096]{1,0:T(8,128)} copy-done((f32[512,4096]{1,0:T(8,128)}, f32[512,4096]{1,0:T(8,128)S(1)}, u32[]{:S(2)}) %copy-start) | copy-done | bytes 8388632
  72.1 0.0 copy-done.1
  72.1 8.9 %convolution_multiply_fusion.1 = f32[512,64]{0,1:T(8,128)} fusion(f32[512,4096]{1,0:T(8,128)S(1)} %subtract_select_fusion, f32[4096,64]{0,1:T(8,128)S(1)} %copy-done.1), kind=kOutput, calls=%fused_computation.3 | convolution fusion | flops 1610645504 | bytes 9568256 | tf_op jit(solution)/shard_map/dot_general | solution.py:33
  81.0 0.0 reduce-scatter.3.cloned.1.call-update
  81.1 0.2 reduce-scatter.5.cloned.1.call-start
  81.3 9.0 %convolution_multiply_fusion = f32[4096,64]{0,1:T(8,128)} fusion(f32[512,4096]{1,0:T(8,128)} %copy-done, f32[512,64]{0,1:T(8,128)S(1)} %reduce_sum.9), kind=kOutput, calls=%fused_computation.2 | convolution fusion | flops 1610874880 | bytes 9568256 | tf_op jit(solution)/shard_map/ij,ik->jk/dot_general | solution.py:40
  90.3 0.0 reduce-scatter.5.cloned.1.call-update
  90.3 0.9 reduce-scatter.3.cloned.1.call-done
  91.2 61.8 %reduce-scatter.5.cloned.1.call-done = f32[256,64]{0,1:T(8,128)} async-done(((f32[4096,64]{0,1:T(8,128)}), f32[256,64]{0,1:T(8,128)}) %reduce-scatter.5.cloned.1.call-update) | async-done | bytes 65552 | tf_op jit(solution)/shard_map/reduce_scatter | solution.py:39
  (2 shorter events, 0.0 us)
Async XLA Ops:
  7.2 42.4 %all-gather.3.cloned.1.call-start = ((), (), s32[]{:S(2)}) async-start(), calls=%async_computation.2 | async-start | bytes 1114112 | tf_op jit(solution)/shard_map/all_gather | solution.py:21
  7.9 83.3 %reduce-scatter.3.cloned.1.call-start = ((), (), s32[]{:S(2)}) async-start(), calls=%async_computation.3 | async-start | bytes 196608 | tf_op jit(solution)/shard_map/reduce_scatter | solution.py:32
  57.3 14.8 %copy-start.1 = (f32[4096,64]{0,1:T(8,128)S(1)}, f32[4096,64]{0,1:T(8,128)}, u32[]{:S(2)}) copy-start(f32[4096,64]{0,1:T(8,128)} %all-gather.3.cloned.1.call-done) | copy-start | bytes 3145732
  68.9 3.2 %copy-start = (f32[512,4096]{1,0:T(8,128)}, f32[512,4096]{1,0:T(8,128)S(1)}, u32[]{:S(2)}) copy-start(f32[512,4096]{1,0:T(8,128)S(1)} %subtract_select_fusion) | copy-start | bytes 25165828
  81.1 72.0 %reduce-scatter.5.cloned.1.call-start = ((), (), s32[]{:S(2)}) async-start(), calls=%async_computation.4 | async-start | bytes 1114112 | tf_op jit(solution)/shard_map/reduce_scatter | solution.py:39
Sparse Core Ops, SparseCore 0:
  10.1 39.3 all-gather.2
  81.2 9.9 reduce-scatter.2
  95.4 57.6 reduce-scatter.4
